TPU v7x, 32 devices: a whole 2x2x4 slice. The times are simulated.
32 devices in a mesh: shard: 4 (over z), ctx: 4 (over x, core), tp: 2 (over y).
Axes of the slice: x: 2, y: 2, z: 4, core: 2. Of those that a mesh axis runs over, the one named last changes fastest.
Arguments:
- layer_in: bfloat16 [3072, 2048], P(('shard', 'ctx')), may hold values from -6 to 6
- w_qkv: bfloat16 [6144, 2048], P(('shard', 'ctx'), 'tp'), may hold values from -0.125 to 0.125
- w_out: bfloat16 [2048, 2048], P(('shard', 'ctx'), 'tp'), may hold values from -1.5 to 1.5
- norm_gains: bfloat16 [2048, 4], P(('shard', 'ctx')), may hold values from 0.25 to 1.75
- router: bfloat16 [2048, 16], P(('shard', 'ctx')), may hold values from -0.0625 to 0.0625
- w_gate_up: bfloat16 [16, 2048, 2, 1024], P(('shard', 'ctx'), None, None, 'tp'), may hold values from -0.125 to 0.125
- w_down: bfloat16 [16, 2048, 1024], P(('shard', 'ctx'), None, 'tp'), may hold values from -0.75 to 0.75
- routes: int32 [3072, 8], P(('shard', 'ctx')), may hold values from 0 to 15, all different within a row; in each aligned block of 192 rows (0 to 191, 192 to 383, ...) at most 120 rows name the same one
- lengths: int32 [4, 3], P('shard'), may hold values from 1 to 614, 768 in all within a row
- token_order: int32 [4, 768], P('shard'), may hold values from 0 to 767, each once within a row
- out_grad: bfloat16 [3072, 2048], P(('shard', 'ctx')), may hold values from -6 to 6
Outputs:
- output: bfloat16 [3072, 2048], P(('shard', 'ctx'))
- input_grad: float32 [3072, 2048], P(('shard', 'ctx'))
- qkv_grad: float32 [6144, 2048], P(('shard', 'ctx'), 'tp')
- out_proj_grad: float32 [2048, 2048], P(('shard', 'ctx'), 'tp')
- gains_grad: float32 [2048, 4], P(('shard', 'ctx'))
- router_grad: float32 [2048, 16], P(('shard', 'ctx'))
- gate_up_grad: float32 [16, 2048, 2, 1024], P(('shard', 'ctx'), None, None, 'tp')
- down_grad: float32 [16, 2048, 1024], P(('shard', 'ctx'), None, 'tp')
Inputs may be any that keep to these rules, and one draw needn't show every extreme that they name: `routes`: each row names 8 different experts. Among the 192 rows of one device no expert is named more than 120 times, a bound that some block reaches there. Each row holds the lengths of the 3 sequences of one group; they sum to 768 and the longest is exactly 614. `token_order`: each row is a permutation of the places of its group.
All inputs are finite; a program needn't handle non-finite values.
Results may differ from a plain program's by a relative error of at most 0.017.
Values may be sent and summed in bfloat16 or wider, within the bound.
No kernel may reach another device: no remote copies, remote signals or barrier semaphores. Data moves between devices by JAX's collectives and lax.ppermute only.
A program may use at most 320 MiB of HBM per device.

v0:
```python
import jax
import jax.numpy as jnp
from jax import lax
from jax.sharding import PartitionSpec as P

HEAD = 128
norm_eps = 1e-05
rope_base = 10000.0
masked_score = -1e30


def places_info(order_row, length_row):
    seq_ends = jnp.cumsum(length_row)
    seq_starts = seq_ends - length_row
    sequence = jnp.sum((order_row[:, None] >= seq_ends[None, :]).astype(jnp.int32), axis=1)
    picker = jnp.arange(length_row.shape[0], dtype=jnp.int32)[None, :] == sequence[:, None]
    first_place = jnp.sum(jnp.where(picker, seq_starts[None, :], 0), axis=1)
    return (sequence, order_row - first_place)


def rope_tables(place_pos, head_size):
    freq_index = jnp.arange(head_size // 2, dtype=jnp.float32)
    inverse = 1.0 / rope_base ** (freq_index * 2.0 / head_size)
    angle = place_pos.astype(jnp.float32)[:, None] * inverse[None, :]
    cosine = jnp.cos(angle)
    sine = jnp.sin(angle)
    return (jnp.concatenate([cosine, cosine], 1), jnp.concatenate([sine, sine], 1))


def rotate(values_in, cosine, sine):
    half_width = values_in.shape[-1] // 2
    turned = jnp.concatenate([-values_in[..., half_width:], values_in[..., :half_width]], -1)
    return values_in * cosine[:, None, :] + turned * sine[:, None, :]


def rotate_back(grad_in, cosine, sine):
    half_width = grad_in.shape[-1] // 2
    scaled = grad_in * sine[:, None, :]
    return grad_in * cosine[:, None, :] + jnp.concatenate(
        [scaled[..., half_width:], -scaled[..., :half_width]], -1
    )


def slot_index(expert_flat, expert_count, capacity):
    chosen = (expert_flat[:, None] == jnp.arange(expert_count, dtype=jnp.int32)[None, :]).astype(
        jnp.int32
    )
    before = jnp.cumsum(chosen, axis=0) - chosen
    slot_num = jnp.sum(before * chosen, axis=1)
    return expert_flat * capacity + slot_num


def local(
    layer_in,
    w_qkv,
    w_out,
    norm_gains,
    router,
    w_gate_up,
    w_down,
    routes,
    lengths,
    token_order,
    out_grad,
):
    tokens, width = layer_in.shape
    topk = routes.shape[1]
    experts = router.shape[1]
    capacity = max(2, tokens * topk * 5 // (4 * experts))
    qkv_all, out_all, gains_all, router_all = (
        lax.all_gather(w_qkv, ("shard", "ctx"), axis=0, tiled=True),
        lax.all_gather(w_out, ("shard", "ctx"), axis=0, tiled=True),
        lax.all_gather(norm_gains, ("shard", "ctx"), axis=0, tiled=True),
        lax.all_gather(router, ("shard", "ctx"), axis=0, tiled=True),
    )
    half_width = qkv_all.shape[1]
    full_heads = half_width * lax.axis_size("tp")
    head_count = half_width // HEAD
    tp_index = lax.axis_index("tp")
    ctx_index = lax.axis_index("ctx")
    gains_f = gains_all.astype(jnp.float32)
    gain_in = gains_f[:, 0]
    gain_mid = gains_f[:, 1]
    gain_q = lax.dynamic_slice_in_dim(gains_f[:, 2], tp_index * half_width, half_width)
    gain_k = lax.dynamic_slice_in_dim(gains_f[:, 3], tp_index * half_width, half_width)
    score_scale = HEAD ** (-0.5)
    group_len = token_order.shape[1]
    seq_all, pos_all = places_info(token_order[0], lengths[0])
    seq_mine = lax.dynamic_slice_in_dim(seq_all, ctx_index * tokens, tokens)
    pos_mine = lax.dynamic_slice_in_dim(pos_all, ctx_index * tokens, tokens)
    cosine, sine = rope_tables(pos_mine, HEAD)
    visible = (seq_mine[:, None] == seq_all[None, :]) & (pos_all[None, :] <= pos_mine[:, None])
    layer_f = layer_in.astype(jnp.float32)
    rate_in = lax.rsqrt(jnp.mean(layer_f * layer_f, axis=-1, keepdims=True) + norm_eps)
    in_hat = layer_f * rate_in
    in_norm = in_hat * gain_in
    in_low = in_norm.astype(jnp.bfloat16)
    qkv_mats = qkv_all.reshape(3, width, half_width)
    projected = jnp.einsum("td,jdh->tjh", in_low, qkv_mats, preferred_element_type=jnp.float32)
    q_raw = projected[:, 0]
    k_raw = projected[:, 1]
    v_raw = projected[:, 2]
    square_q, square_k = lax.psum(
        (jnp.sum(q_raw * q_raw, axis=1), jnp.sum(k_raw * k_raw, axis=1)), "tp"
    )
    rate_q = lax.rsqrt(square_q / full_heads + norm_eps)[:, None]
    rate_k = lax.rsqrt(square_k / full_heads + norm_eps)[:, None]
    q_hat = q_raw * rate_q
    k_hat = k_raw * rate_k
    q_low = rotate((q_hat * gain_q).reshape(tokens, head_count, HEAD), cosine, sine).astype(
        jnp.bfloat16
    )
    k_low = (
        rotate((k_hat * gain_k).reshape(tokens, head_count, HEAD), cosine, sine)
        .astype(jnp.bfloat16)
        .reshape(tokens, half_width)
    )
    v_low = v_raw.astype(jnp.bfloat16)
    key_rows, value_rows = (
        lax.all_gather(k_low, "ctx", axis=0, tiled=True),
        lax.all_gather(v_low, "ctx", axis=0, tiled=True),
    )
    key_heads = key_rows.reshape(group_len, head_count, HEAD)
    value_heads = value_rows.reshape(group_len, head_count, HEAD)
    scores = (
        jnp.einsum("qhd,khd->hqk", q_low, key_heads, preferred_element_type=jnp.float32)
        * score_scale
    )
    scores = jnp.where(visible[None], scores, masked_score)
    row_max = jnp.max(scores, axis=-1, keepdims=True)
    shifted = jnp.exp(scores - row_max)
    row_sum = jnp.sum(shifted, axis=-1, keepdims=True)
    weights = shifted / row_sum
    log_total = row_max + jnp.log(row_sum)
    mixed = jnp.einsum(
        "hqk,khd->qhd",
        weights.astype(jnp.bfloat16),
        value_heads,
        preferred_element_type=jnp.float32,
    )
    mixed_low = mixed.reshape(tokens, half_width).astype(jnp.bfloat16)
    attn_part = lax.dot_general(
        mixed_low, out_all, (((1,), (1,)), ((), ())), preferred_element_type=jnp.float32
    )
    attn = lax.psum(attn_part, "tp")
    resid = layer_f + attn
    rate_mid = lax.rsqrt(jnp.mean(resid * resid, axis=-1, keepdims=True) + norm_eps)
    mid_hat = resid * rate_mid
    mid_norm = mid_hat * gain_mid
    mid_low = mid_norm.astype(jnp.bfloat16)
    router_f = router_all.astype(jnp.float32)
    logits = jnp.dot(mid_norm, router_f, precision=lax.Precision.HIGHEST)
    chosen = routes[:, :, None] == jnp.arange(experts, dtype=jnp.int32)[None, None, :]
    picked = jnp.sum(jnp.where(chosen, logits[:, None, :], 0.0), axis=-1)
    picked_max = jnp.max(picked, axis=-1, keepdims=True)
    picked_exp = jnp.exp(picked - picked_max)
    gates = picked_exp / jnp.sum(picked_exp, axis=-1, keepdims=True)
    slot_dest = slot_index(routes.reshape(-1), experts, capacity)
    token_of = jnp.arange(tokens * topk, dtype=jnp.int32) // topk
    slot_token = jnp.full((experts * capacity,), -1, jnp.int32).at[slot_dest].set(token_of)
    filled = slot_token >= 0
    safe_token = jnp.maximum(slot_token, 0)
    gate_slot = jnp.zeros((experts * capacity,), jnp.float32).at[slot_dest].set(gates.reshape(-1))
    send_mid = jnp.where(filled[:, None], mid_low[safe_token], jnp.zeros((), jnp.bfloat16)).reshape(
        experts, capacity, width
    )
    send_grad = (
        (gate_slot[:, None] * out_grad[safe_token].astype(jnp.float32))
        .astype(jnp.bfloat16)
        .reshape(experts, capacity, width)
    )
    recv_mid, recv_grad = (
        lax.all_to_all(send_mid, ("shard", "ctx"), split_axis=0, concat_axis=1, tiled=True),
        lax.all_to_all(send_grad, ("shard", "ctx"), split_axis=0, concat_axis=1, tiled=True),
    )
    gate_up = jnp.einsum("erd,edjf->erjf", recv_mid, w_gate_up, preferred_element_type=jnp.float32)
    gate_val = gate_up[:, :, 0]
    up_val = gate_up[:, :, 1]
    gate_sig = jax.nn.sigmoid(gate_val)
    gate_act = gate_val * gate_sig
    hidden_act = (gate_act * up_val).astype(jnp.bfloat16)
    expert_part = jnp.einsum("erf,edf->erd", hidden_act, w_down, preferred_element_type=jnp.float32)
    hidden_grad = jnp.einsum("erd,edf->erf", recv_grad, w_down, preferred_element_type=jnp.float32)
    gate_grad = hidden_grad * up_val * gate_sig * (1.0 + gate_val * (1.0 - gate_sig))
    up_grad = hidden_grad * gate_act
    both_grad = jnp.stack([gate_grad, up_grad], axis=2).astype(jnp.bfloat16)
    mid_part = jnp.einsum(
        "erjf,edjf->erd", both_grad, w_gate_up, preferred_element_type=jnp.float32
    )
    gate_up_grad = jnp.einsum(
        "erd,erjf->edjf", recv_mid, both_grad, preferred_element_type=jnp.float32
    )
    down_grad = jnp.einsum(
        "erd,erf->edf", recv_grad, hidden_act, preferred_element_type=jnp.float32
    )
    out_grad_f = out_grad.astype(jnp.float32)
    back_rows, back_grads = (
        lax.all_to_all(expert_part, ("shard", "ctx"), split_axis=1, concat_axis=0, tiled=True),
        lax.all_to_all(mid_part, ("shard", "ctx"), split_axis=1, concat_axis=0, tiled=True),
    )
    columns = back_rows.shape[-1]
    rows_y = back_rows.reshape(experts * capacity, columns)[slot_dest].reshape(
        tokens, topk, columns
    )
    rows_g = back_grads.reshape(experts * capacity, columns)[slot_dest].reshape(
        tokens, topk, columns
    )
    mixture_part = jnp.sum(gates[:, :, None] * rows_y, axis=1)
    grad_part = jnp.sum(rows_g, axis=1)
    score_part = jnp.sum(out_grad_f[:, None, :] * rows_y, axis=2)
    mixture_part, grad_part, score_part = (mixture_part, grad_part, score_part)
    mixture, mid_grad, score_total = lax.psum((mixture_part, grad_part, score_part), "tp")
    output = (resid + mixture).astype(jnp.bfloat16)
    picked_grad = gates * (score_total - jnp.sum(gates * score_total, axis=1, keepdims=True))
    logit_grad = jnp.sum(jnp.where(chosen, picked_grad[:, :, None], 0.0), axis=1)
    router_grad = lax.dot_general(
        mid_norm, logit_grad, (((0,), (0,)), ((), ())), precision=lax.Precision.HIGHEST
    )
    mid_grad = mid_grad + lax.dot_general(
        logit_grad, router_f, (((1,), (1,)), ((), ())), precision=lax.Precision.HIGHEST
    )
    mid_scaled = gain_mid * mid_grad
    resid_grad = out_grad_f + rate_mid * (
        mid_scaled - mid_hat * jnp.mean(mid_hat * mid_scaled, axis=-1, keepdims=True)
    )
    gain_mid_grad = jnp.sum(mid_grad * mid_hat, axis=0)
    attn_low = resid_grad.astype(jnp.bfloat16)
    out_proj_grad = lax.dot_general(
        attn_low, mixed_low, (((0,), (0,)), ((), ())), preferred_element_type=jnp.float32
    )
    mixed_grad = (
        jnp.dot(attn_low, out_all, preferred_element_type=jnp.float32)
        .astype(jnp.bfloat16)
        .reshape(tokens, head_count, HEAD)
    )
    again = (
        jnp.einsum("qhd,khd->hqk", q_low, key_heads, preferred_element_type=jnp.float32)
        * score_scale
    )
    again = jnp.where(visible[None], again, masked_score)
    weights_again = jnp.exp(again - log_total)
    weights_low = weights_again.astype(jnp.bfloat16)
    weight_grad = jnp.einsum(
        "qhd,khd->hqk", mixed_grad, value_heads, preferred_element_type=jnp.float32
    )
    score_grad = weights_again * (
        weight_grad - jnp.sum(weights_again * weight_grad, axis=-1, keepdims=True)
    )
    score_low = score_grad.astype(jnp.bfloat16)
    q_grad = (
        jnp.einsum("hqk,khd->qhd", score_low, key_heads, preferred_element_type=jnp.float32)
        * score_scale
    )
    k_part = (
        jnp.einsum("hqk,qhd->khd", score_low, q_low, preferred_element_type=jnp.float32)
        * score_scale
    )
    v_part = jnp.einsum("hqk,qhd->khd", weights_low, mixed_grad, preferred_element_type=jnp.float32)
    k_grad, v_grad = (
        lax.psum_scatter(
            k_part.reshape(group_len, half_width), "ctx", scatter_dimension=0, tiled=True
        ),
        lax.psum_scatter(
            v_part.reshape(group_len, half_width), "ctx", scatter_dimension=0, tiled=True
        ),
    )
    q_in = rotate_back(q_grad, cosine, sine).reshape(tokens, half_width)
    k_in = rotate_back(k_grad.reshape(tokens, head_count, HEAD), cosine, sine).reshape(
        tokens, half_width
    )
    q_scaled = gain_q * q_in
    k_scaled = gain_k * k_in
    inner_q, inner_k = lax.psum(
        (jnp.sum(q_scaled * q_hat, axis=1), jnp.sum(k_scaled * k_hat, axis=1)), "tp"
    )
    q_raw_grad = rate_q * (q_scaled - q_hat * (inner_q / full_heads)[:, None])
    k_raw_grad = rate_k * (k_scaled - k_hat * (inner_k / full_heads)[:, None])
    gain_pair = jnp.stack([jnp.sum(q_in * q_hat, axis=0), jnp.sum(k_in * k_hat, axis=0)], axis=1)
    qk_gain_part = lax.dynamic_update_slice(
        jnp.zeros((width, 2), jnp.float32), gain_pair, (tp_index * half_width, 0)
    )
    raw_grad = jnp.stack([q_raw_grad, k_raw_grad, v_grad], axis=1).astype(jnp.bfloat16)
    qkv_grad = jnp.einsum(
        "td,tjh->jdh", in_low, raw_grad, preferred_element_type=jnp.float32
    ).reshape(3 * width, half_width)
    norm_part = jnp.einsum("tjh,jdh->td", raw_grad, qkv_mats, preferred_element_type=jnp.float32)
    in_norm_grad, qk_gain_grad = (
        lax.psum(norm_part.astype(jnp.bfloat16), "tp").astype(jnp.float32),
        lax.psum(qk_gain_part.astype(jnp.bfloat16), "tp").astype(jnp.float32),
    )
    in_scaled = gain_in * in_norm_grad
    input_grad = resid_grad + rate_in * (
        in_scaled - in_hat * jnp.mean(in_hat * in_scaled, axis=-1, keepdims=True)
    )
    gain_in_grad = jnp.sum(in_norm_grad * in_hat, axis=0)
    gains_grad = jnp.stack(
        [gain_in_grad, gain_mid_grad, qk_gain_grad[:, 0], qk_gain_grad[:, 1]], axis=1
    )
    qkv_owned, out_owned, gains_owned, router_owned = (
        lax.psum_scatter(qkv_grad, ("shard", "ctx"), scatter_dimension=0, tiled=True),
        lax.psum_scatter(out_proj_grad, ("shard", "ctx"), scatter_dimension=0, tiled=True),
        lax.psum_scatter(gains_grad, ("shard", "ctx"), scatter_dimension=0, tiled=True),
        lax.psum_scatter(router_grad, ("shard", "ctx"), scatter_dimension=0, tiled=True),
    )
    return (
        output,
        input_grad,
        qkv_owned,
        out_owned,
        gains_owned,
        router_owned,
        gate_up_grad,
        down_grad,
    )


def solution(mesh):
    in_specs = (
        P(("shard", "ctx"), None),
        P(("shard", "ctx"), "tp"),
        P(("shard", "ctx"), "tp"),
        P(("shard", "ctx"), None),
        P(("shard", "ctx"), None),
        P(("shard", "ctx"), None, None, "tp"),
        P(("shard", "ctx"), None, "tp"),
        P(("shard", "ctx"), None),
        P("shard", None),
        P("shard", None),
        P(("shard", "ctx"), None),
    )
    out_specs = (
        P(("shard", "ctx"), None),
        P(("shard", "ctx"), None),
        P(("shard", "ctx"), "tp"),
        P(("shard", "ctx"), "tp"),
        P(("shard", "ctx"), None),
        P(("shard", "ctx"), None),
        P(("shard", "ctx"), None, None, "tp"),
        P(("shard", "ctx"), None, "tp"),
    )
    return jax.shard_map(local, mesh=mesh, in_specs=in_specs, out_specs=out_specs, check_vma=False)
```

profile of v0, /device:TPU:0, one launch (start us, length us, event | category | flops | bytes accessed | tf_op | source)
XLA Modules:
  0.0 2155.8 jit_solution(1457848799466026686)
XLA Ops:
  10.4 23.8 %all_gather.18 = bf16[2048,4]{0,1:T(4,128)(2,1)S(1)} all-gather(bf16[128,4]{0,1:T(4,128)(2,1)} %param.14), channel_id=1, replica_groups=mesh['shard'=4,'ctx'=4,'tp'=2] {'shard','ctx'}, dimensions={0}, use_global_device_ids=true | all-gather | bytes 17408 | tf_op jit(solution)/shard_map/all_gather | solution.py:73
  37.0 76.5 %all-gather.6.cloned.1.call-done = bf16[6144,1024]{1,0:T(8,128)(2,1)} async-done(((bf16[384,1024]{1,0:T(8,128)(2,1)}), bf16[6144,1024]{1,0:T(8,128)(2,1)}) %all-gather.6.cloned.1.call-update) | async-done | bytes 12582928 | tf_op jit(solution)/shard_map/all_gather | solution.py:71
  113.5 6.1 fusion.78
  126.8 4.9 all-reduce.1
  140.6 3.0 copy.170
  143.6 18.0 all-gather.8.cloned.1.call-done
  161.6 2.6 fusion.117
  168.4 45.7 %all-gather.10.cloned.1.call-done = bf16[2048,1024]{1,0:T(8,128)(2,1)} async-done(((bf16[128,1024]{1,0:T(8,128)(2,1)}), bf16[2048,1024]{1,0:T(8,128)(2,1)}) %all-gather.10.cloned.1.call-update) | async-done | bytes 4194320 | tf_op jit(solution)/shard_map/all_gather | solution.py:72
  214.1 4.9 fusion.83
  219.6 4.5 reduce-window.11
  224.9 6.4 scatter_custom_fusion
  231.5 37.7 %all-reduce.7.cloned.1.call-done = f32[192,2048]{1,0:T(8,128)} async-done(((f32[192,2048]{1,0:T(8,128)}), f32[192,2048]{1,0:T(8,128)}) %all-reduce.7.cloned.1.call-update) | async-done | bytes 1572880 | tf_op jit(solution)/shard_map/psum | solution.py:145
  272.2 8.6 gather_fusion
  280.9 7.1 broadcast_select_fusion
  288.0 5.8 all-to-all-start
  293.8 8.7 gather_fusion.2
  302.5 134.7 %all_gather.23 = bf16[2048,16]{0,1:T(8,128)(2,1)S(1)} all-gather(bf16[128,16]{0,1:T(8,128)(2,1)S(1)} %copy-done.70), channel_id=1, replica_groups=mesh['shard'=4,'ctx'=4,'tp'=2] {'shard','ctx'}, dimensions={0}, use_global_device_ids=true | all-gather | bytes 69632 | tf_op jit(solution)/shard_map/all_gather | solution.py:74
  437.9 2.4 fusion.49
  441.7 6.2 scatter_custom_fusion.1
  448.0 7.7 fusion
  455.7 42.1 %all-to-all-start.2 = ((bf16[16,120,2048]{2,1,0:T(8,128)(2,1)}), bf16[16,120,2048]{2,1,0:T(8,128)(2,1)}, u32[]{:S(2)}, u32[]{:S(2)}) async-start(bf16[16,120,2048]{2,1,0:T(8,128)(2,1)} %fusion), calls=%async_computation.2 | async-start | bytes 15728640 | tf_op jit(solution)/shard_map/all_to_all | solution.py:174
  497.8 13.8 convolution_bitcast_fusion.4
  511.6 127.7 %all-to-all-done.2 = bf16[16,120,2048]{2,1,0:T(8,128)(2,1)} async-done(((bf16[16,120,2048]{2,1,0:T(8,128)(2,1)}), bf16[16,120,2048]{2,1,0:T(8,128)(2,1)}, u32[]{:S(2)}, u32[]{:S(2)}) %all-to-all-start.2) | async-done | bytes 7864352 | tf_op jit(solution)/shard_map/all_to_all | solution.py:174
  639.3 12.0 fusion.31
  651.3 10.6 convolution_bitcast_fusion
  662.0 22.7 %copy.137 = f32[1,1920,2048]{2,0,1:T(1,128)} copy(f32[1,1920,2048]{2,1,0:T(8,128)S(1)} %convolution_bitcast_fusion) | data formatting | bytes 31457280 | tf_op jit(solution)/shard_map/erjf,edjf->erd/dot_general | solution.py:187
  684.6 35.3 %all-to-all-start.3 = ((f32[1,1920,2048]{2,0,1:T(1,128)}), f32[1,1920,2048]{2,0,1:T(1,128)}, u32[]{:S(2)}, u32[]{:S(2)}) async-start(f32[1,1920,2048]{2,0,1:T(1,128)} %copy.137), calls=%async_computation.3 | async-start | bytes 31457280 | tf_op jit(solution)/shard_map/all_to_all | solution.py:199
  719.9 4.6 multiply_convert_fusion.1
  724.5 4.3 convolution_bitcast_fusion.1
  728.8 22.6 %copy.134 = f32[1,1920,2048]{2,0,1:T(1,128)} copy(f32[1,1920,2048]{2,1,0:T(8,128)S(1)} %convolution_bitcast_fusion.1) | data formatting | bytes 31457280 | tf_op jit(solution)/shard_map/erf,edf->erd/dot_general | solution.py:182
  751.5 246.8 %all-to-all-done.3 = f32[1,1920,2048]{2,0,1:T(1,128)} async-done(((f32[1,1920,2048]{2,0,1:T(1,128)}), f32[1,1920,2048]{2,0,1:T(1,128)}, u32[]{:S(2)}, u32[]{:S(2)}) %all-to-all-start.3) | async-done | bytes 15728672 | tf_op jit(solution)/shard_map/all_to_all | solution.py:199
  998.3 66.0 %all-to-all-start.1 = ((f32[1,1920,2048]{2,0,1:T(1,128)}), f32[1,1920,2048]{2,0,1:T(1,128)}, u32[]{:S(2)}, u32[]{:S(2)}) async-start(f32[1,1920,2048]{2,0,1:T(1,128)} %copy.134), calls=%async_computation.1 | async-start | bytes 31457280 | tf_op jit(solution)/shard_map/all_to_all | solution.py:198
  1064.8 18.7 copy.240
  1083.5 18.4 gather_fusion.3
  1101.9 8.7 bitcast_reduce_fusion
  1110.6 232.1 %all-to-all-done.1 = f32[1,1920,2048]{2,0,1:T(1,128)} async-done(((f32[1,1920,2048]{2,0,1:T(1,128)}), f32[1,1920,2048]{2,0,1:T(1,128)}, u32[]{:S(2)}, u32[]{:S(2)}) %all-to-all-start.1) | async-done | bytes 15728672 | tf_op jit(solution)/shard_map/all_to_all | solution.py:198
  1342.7 18.9 copy.241
  1361.6 18.2 gather_fusion.1
  1379.8 8.6 fusion.2
  1389.1 5.1 psum.75
  1394.3 140.6 %all-reduce.11.cloned.1.call-done = (f32[192,2048]{1,0:T(8,128)}, f32[192,2048]{1,0:T(8,128)}) async-done(((f32[192,2048]{1,0:T(8,128)}, f32[192,2048]{1,0:T(8,128)}), (f32[192,2048]{1,0:T(8,128)}, f32[192,2048]{1,0:T(8,128)})) %all-reduce.11.cloned.1.call-update) | async-done | bytes 3145744 | tf_op jit(solution)/shard_map/psum | solution.py:212
  1534.9 2.8 multiply_reduce_fusion.1
  1541.9 3.6 multiply_reduce_fusion
  1546.6 2.4 convolution_multiply_fusion
  1549.1 3.5 copy.152
  1552.7 5.0 fusion.21
  1557.7 3.7 copy.153
  1562.3 3.0 broadcast_multiply_fusion
  1568.6 22.1 %reduce-scatter.9.cloned.1.call-done = f32[192,1024]{1,0:T(8,128)} async-done(((f32[768,1024]{1,0:T(8,128)}), f32[192,1024]{1,0:T(8,128)}) %reduce-scatter.9.cloned.1.call-update) | async-done | bytes 786448 | tf_op jit(solution)/shard_map/reduce_scatter | solution.py:260
  1592.2 2.6 multiply_reduce_fusion.4
  1594.8 5.0 all-reduce
  1602.9 28.7 %reduce-scatter.11.cloned.1.call-done = f32[192,1024]{1,0:T(8,128)} async-done(((f32[768,1024]{1,0:T(8,128)}), f32[192,1024]{1,0:T(8,128)}) %reduce-scatter.11.cloned.1.call-update) | async-done | bytes 786448 | tf_op jit(solution)/shard_map/reduce_scatter | solution.py:263
  1633.6 9.8 fusion.16
  1643.5 5.0 psum.79
  1648.5 29.4 %all-reduce.9.cloned.1.call-done = bf16[192,2048]{1,0:T(8,128)(2,1)} async-done(((bf16[192,2048]{1,0:T(8,128)(2,1)}), bf16[192,2048]{1,0:T(8,128)(2,1)}) %all-reduce.9.cloned.1.call-update) | async-done | bytes 786448 | tf_op jit(solution)/shard_map/psum | solution.py:288
  1683.1 5.9 fusion.81
  1690.1 10.4 convolution_bitcast_fusion.2
  1700.5 24.7 %copy.148 = f32[3,2048,1024]{2,1,0:T(8,128)} copy(f32[3,2048,1024]{1,2,0:T(8,128)} %convolution_bitcast_fusion.2) | data formatting | bytes 50331648 | tf_op jit(solution)/shard_map/td,tjh->jdh/transpose | solution.py:283
  1726.8 12.1 convolution_bitcast_fusion.3
  1738.9 16.5 copy.150
  1755.4 9.6 convolution_bitcast_fusion.5
  1768.2 25.7 %reduce-scatter.17.cloned.1.call-done = f32[128,16]{0,1:T(8,128)} async-done(((f32[2048,16]{0,1:T(8,128)}), f32[128,16]{0,1:T(8,128)}) %reduce-scatter.17.cloned.1.call-update) | async-done | bytes 8208 | tf_op jit(solution)/shard_map/reduce_scatter | solution.py:303
  1793.9 107.1 %reduce-scatter.15.cloned.1.call-done = f32[128,1024]{1,0:T(8,128)} async-done(((f32[2048,1024]{1,0:T(8,128)}), f32[128,1024]{1,0:T(8,128)}) %reduce-scatter.15.cloned.1.call-update) | async-done | bytes 524304 | tf_op jit(solution)/shard_map/reduce_scatter | solution.py:301
  1900.9 247.9 %reduce-scatter.13.cloned.1.call-done = f32[384,1024]{1,0:T(8,128)} async-done(((f32[6144,1024]{1,0:T(8,128)}), f32[384,1024]{1,0:T(8,128)}) %reduce-scatter.13.cloned.1.call-update) | async-done | bytes 1572880 | tf_op jit(solution)/shard_map/reduce_scatter | solution.py:300
  (271 shorter events, 60.8 us)
Async XLA Ops:
  7.2 632.1 %copy-start = (bf16[1,2048,512]{2,1,0:T(8,128)(2,1)S(1)}, bf16[1,2048,512]{2,1,0:T(8,128)(2,1)}, u32[]{:S(2)}) copy-start(bf16[1,2048,512]{2,1,0:T(8,128)(2,1)} %param.17) | copy-start | bytes 6291460
  7.2 106.3 %copy-start.7 = (bf16[192,2048]{1,0:T(8,128)(2,1)S(1)}, bf16[192,2048]{1,0:T(8,128)(2,1)}, u32[]{:S(2)}) copy-start(bf16[192,2048]{1,0:T(8,128)(2,1)} %param.11) | copy-start | bytes 2359300
  7.2 106.3 %all-gather.6.cloned.1.call-start = ((), (), s32[]{:S(2)}) async-start(), calls=%async_computation.10 | async-start | bytes 13369344 | tf_op jit(solution)/shard_map/all_gather | solution.py:71
  7.9 132.7 %all-gather.12.cloned.1.call-start = ((), (), s32[]{:S(2)}) async-start(), calls=%async_computation.20 | async-start | bytes 1966080 | tf_op jit(solution)/shard_map/all_gather | solution.py:121
  35.5 99.5 %copy-start.35 = (f32[192,128]{1,0:T(8,128)}, f32[192,128]{1,0:T(8,128)S(1)}, u32[]{:S(2)}) copy-start(f32[192,128]{1,0:T(8,128)S(1)} %get-tuple-element.88) | copy-start | bytes 294916
  37.0 82.6 %copy-start.55 = (f32[192]{0:T(256)}, f32[192]{0:T(256)S(1)}, u32[]{:S(2)}) copy-start(f32[192]{0:T(256)S(1)} %add_rsqrt_fusion.3) | copy-start | bytes 2308
  37.0 82.6 %copy-start.39 = (f32[2048,1]{0,1:T(1,128)}, f32[2048,1]{0,1:T(1,128)S(1)}, u32[]{:S(2)}) copy-start(f32[2048,1]{0,1:T(1,128)S(1)} %get-tuple-element.94) | copy-start | bytes 24580
  37.0 400.2 %copy-start.43 = (f32[2048,1]{0,1:T(1,128)}, f32[2048,1]{0,1:T(1,128)S(1)}, u32[]{:S(2)}) copy-start(f32[2048,1]{0,1:T(1,128)S(1)} %get-tuple-element.91) | copy-start | bytes 24580
  121.8 39.8 %all-gather.8.cloned.1.call-start = ((), (), s32[]{:S(2)}) async-start(), calls=%async_computation.11 | async-start | bytes 1966080 | tf_op jit(solution)/shard_map/all_gather | solution.py:120
  121.9 13.2 copy-start.49
  121.9 14.6 copy-start.51
  131.7 3.3 copy-start.65
  131.7 4.8 copy-start.61
  136.4 25.2 %copy-start.19 = (bf16[192,8,128]{2,0,1:T(8,128)(2,1)}, bf16[192,8,128]{2,0,1:T(8,128)(2,1)S(1)}, u32[]{:S(2)}) copy-start(bf16[192,8,128]{2,0,1:T(8,128)(2,1)S(1)} %get-tuple-element.90) | copy-start | bytes 1179652
  136.4 3.9 copy-start.69
  139.6 74.4 %all-gather.10.cloned.1.call-start = ((), (), s32[]{:S(2)}) async-start(), calls=%async_computation.12 | async-start | bytes 4456448 | tf_op jit(solution)/shard_map/all_gather | solution.py:72
  140.2 129.0 %all-reduce.7.cloned.1.call-start = ((), (), s32[]{:S(2)}) async-start(), calls=%async_computation.13 | async-start | bytes 3145728 | tf_op jit(solution)/shard_map/psum | solution.py:145
  165.6 2.8 copy-start.59
  168.4 50.6 %copy-start.27 = (bf16[8,24,8,128]{3,2,1,0:T(8,128)(2,1)}, bf16[8,24,8,128]{3,2,1,0:T(8,128)(2,1)S(1)}, u32[]{:S(2)}) copy-start(bf16[8,24,8,128]{3,2,1,0:T(8,128)(2,1)S(1)} %fusion.57) | copy-start | bytes 1179652
  168.4 50.6 %copy-start.47 = (s32[192,8]{0,1:T(8,128)S(1)}, s32[192,8]{0,1:T(8,128)}, u32[]{:S(2)}) copy-start(s32[192,8]{0,1:T(8,128)} %param.18) | copy-start | bytes 18436
  270.9 166.3 %copy-start.57 = (f32[192]{0:T(256)}, f32[192]{0:T(256)S(1)}, u32[]{:S(2)}) copy-start(f32[192]{0:T(256)S(1)} %add_rsqrt_fusion) | copy-start | bytes 2308
  287.9 5.8 copy-start.2
  288.0 167.8 %all-to-all-start = ((bf16[16,120,2048]{2,1,0:T(8,128)(2,1)}), bf16[16,120,2048]{2,1,0:T(8,128)(2,1)}, u32[]{:S(2)}, u32[]{:S(2)}) async-start(bf16[16,120,2048]{2,1,0:T(8,128)(2,1)} %broadcast_select_fusion), calls=%async_computation | async-start | bytes 15728640 | tf_op jit(solution)/shard_map/all_to_all | solution.py:173
  293.8 8.8 copy-start.70
  441.6 14.1 copy-start.33
  455.7 183.6 %all-to-all-start.2 = ((bf16[16,120,2048]{2,1,0:T(8,128)(2,1)}), bf16[16,120,2048]{2,1,0:T(8,128)(2,1)}, u32[]{:S(2)}, u32[]{:S(2)}) async-start(bf16[16,120,2048]{2,1,0:T(8,128)(2,1)} %fusion), calls=%async_computation.2 | async-start | bytes 15728640 | tf_op jit(solution)/shard_map/all_to_all | solution.py:174
  639.3 12.0 copy-start.71
  684.6 313.6 %all-to-all-start.3 = ((f32[1,1920,2048]{2,0,1:T(1,128)}), f32[1,1920,2048]{2,0,1:T(1,128)}, u32[]{:S(2)}, u32[]{:S(2)}) async-start(f32[1,1920,2048]{2,0,1:T(1,128)} %copy.137), calls=%async_computation.3 | async-start | bytes 31457280 | tf_op jit(solution)/shard_map/all_to_all | solution.py:199
  724.5 4.3 copy-start.24
  998.3 344.4 %all-to-all-start.1 = ((f32[1,1920,2048]{2,0,1:T(1,128)}), f32[1,1920,2048]{2,0,1:T(1,128)}, u32[]{:S(2)}, u32[]{:S(2)}) async-start(f32[1,1920,2048]{2,0,1:T(1,128)} %copy.134), calls=%async_computation.1 | async-start | bytes 31457280 | tf_op jit(solution)/shard_map/all_to_all | solution.py:198
  1064.3 470.5 %all-reduce.11.cloned.1.call-start = ((), (), s32[]{:S(2)}) async-start(), calls=%async_computation.22 | async-start | bytes 6291456 | tf_op jit(solution)/shard_map/psum | solution.py:212
  1361.6 18.2 copy-start.34
  1388.4 5.8 copy-start.46
  1388.4 5.8 copy-start.64
  1388.4 5.8 copy-start.68
  1388.4 5.9 copy-start.48
  1388.4 146.5 %copy-start.6 = (f32[192,2048]{1,0:T(8,128)S(1)}, f32[192,2048]{1,0:T(8,128)}, u32[]{:S(2)}) copy-start(f32[192,2048]{1,0:T(8,128)} %copy-done.5) | copy-start | bytes 4718596
  1388.4 146.5 %copy-start.38 = (bf16[2048,16]{0,1:T(8,128)(2,1)S(1)}, bf16[2048,16]{0,1:T(8,128)(2,1)}, u32[]{:S(2)}) copy-start(bf16[2048,16]{0,1:T(8,128)(2,1)} %copy-done.37) | copy-start | bytes 196612
  1388.4 146.5 %copy-start.44 = (f32[2048,1]{0,1:T(1,128)S(1)}, f32[2048,1]{0,1:T(1,128)}, u32[]{:S(2)}) copy-start(f32[2048,1]{0,1:T(1,128)} %copy-done.43) | copy-start | bytes 24580
  1388.4 146.4 %copy-start.58 = (f32[192]{0:T(256)S(1)}, f32[192]{0:T(256)}, u32[]{:S(2)}) copy-start(f32[192]{0:T(256)} %copy-done.57) | copy-start | bytes 2308
  1388.5 202.2 %reduce-scatter.9.cloned.1.call-start = ((), (), s32[]{:S(2)}) async-start(), calls=%async_computation.14 | async-start | bytes 3932160 | tf_op jit(solution)/shard_map/reduce_scatter | solution.py:260
  1537.7 2.9 copy-start.12
  1540.5 5.0 slice-start
  1541.9 3.6 slice-start.1
  1552.6 79.0 %reduce-scatter.11.cloned.1.call-start = ((), (), s32[]{:S(2)}) async-start(), calls=%async_computation.15 | async-start | bytes 3932160 | tf_op jit(solution)/shard_map/reduce_scatter | solution.py:263
  1561.4 116.6 %all-reduce.9.cloned.1.call-start = ((), (), s32[]{:S(2)}) async-start(), calls=%async_computation.16 | async-start | bytes 1572864 | tf_op jit(solution)/shard_map/psum | solution.py:288
  1567.1 23.5 %copy-start.36 = (f32[192,128]{1,0:T(8,128)S(1)}, f32[192,128]{1,0:T(8,128)}, u32[]{:S(2)}) copy-start(f32[192,128]{1,0:T(8,128)} %copy-done.35) | copy-start | bytes 294916
  1568.6 23.6 %copy-start.16 = (f32[192,8,128]{2,1,0:T(8,128)S(1)}, f32[192,8,128]{2,1,0:T(8,128)}, u32[]{:S(2)}) copy-start(f32[192,8,128]{2,1,0:T(8,128)} %copy-done.15) | copy-start | bytes 2359300
  1568.6 23.6 %copy-start.52 = (f32[1024,1]{0,1:T(1,128)S(1)}, f32[1024,1]{0,1:T(1,128)}, u32[]{:S(2)}) copy-start(f32[1024,1]{0,1:T(1,128)} %copy-done.51) | copy-start | bytes 12292
  1568.6 23.6 %copy-start.62 = (f32[192]{0:T(256)S(1)}, f32[192]{0:T(256)}, u32[]{:S(2)}) copy-start(f32[192]{0:T(256)} %copy-done.61) | copy-start | bytes 2308
  1594.8 6.7 copy-start.21
  1602.9 40.5 %copy-start.29 = (bf16[192,1,1024]{2,0,1:T(8,128)(2,1)}, bf16[192,1,1024]{2,0,1:T(8,128)(2,1)S(1)}, u32[]{:S(2)}) copy-start(bf16[192,1,1024]{2,0,1:T(8,128)(2,1)S(1)} %multiply_convert_fusion.4) | copy-start | bytes 1179652
  1633.6 44.4 %copy-start.8 = (bf16[192,2048]{1,0:T(8,128)(2,1)S(1)}, bf16[192,2048]{1,0:T(8,128)(2,1)}, u32[]{:S(2)}) copy-start(bf16[192,2048]{1,0:T(8,128)(2,1)} %param.11) | copy-start | bytes 2359300
  1633.6 44.4 %copy-start.40 = (f32[2048,1]{0,1:T(1,128)S(1)}, f32[2048,1]{0,1:T(1,128)}, u32[]{:S(2)}) copy-start(f32[2048,1]{0,1:T(1,128)} %copy-done.39) | copy-start | bytes 24580
  1633.6 44.4 %copy-start.56 = (f32[192]{0:T(256)S(1)}, f32[192]{0:T(256)}, u32[]{:S(2)}) copy-start(f32[192]{0:T(256)} %copy-done.55) | copy-start | bytes 2308
  1643.4 123.3 %reduce-scatter.19.cloned.1.call-start = ((), (), s32[]{:S(2)}) async-start(), calls=%async_computation.21 | async-start | bytes 1114112
  1679.8 3.3 copy-start.28
  1681.2 112.7 %reduce-scatter.17.cloned.1.call-start = ((), (), s32[]{:S(2)}) async-start(), calls=%async_computation.19 | async-start | bytes 139264 | tf_op jit(solution)/shard_map/reduce_scatter | solution.py:303
  1683.0 217.9 %reduce-scatter.15.cloned.1.call-start = ((), (), s32[]{:S(2)}) async-start(), calls=%async_computation.18 | async-start | bytes 8912896 | tf_op jit(solution)/shard_map/reduce_scatter | solution.py:301
  1689.1 459.8 %reduce-scatter.13.cloned.1.call-start = ((), (), s32[]{:S(2)}) async-start(), calls=%async_computation.17 | async-start | bytes 26738688 | tf_op jit(solution)/shard_map/reduce_scatter | solution.py:300
  1738.9 16.5 copy-start.25
  1755.4 9.6 copy-start.10
  1755.4 9.7 copy-start.22
  1765.1 383.7 %copy-start.1 = (bf16[1,2048,512]{2,1,0:T(8,128)(2,1)S(1)}, bf16[1,2048,512]{2,1,0:T(8,128)(2,1)}, u32[]{:S(2)}) copy-start(bf16[1,2048,512]{2,1,0:T(8,128)(2,1)} %param.17) | copy-start | bytes 6291460
  (28 other events, 35.6 us)
Sparse Core Ops, SparseCore 0:
  10.3 103.1 all-gather.5
  121.9 17.8 all-gather.11
  142.0 19.6 all-gather.7
  163.7 50.3 all-gather.9
  219.1 50.0 all-reduce.6
  1388.6 146.2 all-reduce.10
  1552.7 37.8 reduce-scatter.8
  1593.7 37.8 reduce-scatter.10
  1643.5 34.3 all-reduce.8
  1681.4 57.5 reduce-scatter.18
  1743.0 50.8 reduce-scatter.16
  1798.4 102.5 reduce-scatter.14
  1905.6 243.1 reduce-scatter.12
where the time goes:
time: 2170 us; the launch traced here: 2160 us
  waiting for transfers between devices  1390 us (64%)
  local copies, waits for them, and re-layouts  224 us (10%)
  blocking collectives  179 us (8%)
  starting transfers between devices  150 us (7%)
  matrix products  126 us (6%)
  other arithmetic  74.3 us (3%)
    reduce_scatter x1, waiting for transfers between devices, local(): lax.psum_scatter(qkv_grad, ('shard', 'ctx'), scatter_dimension=0, tiled=T...  248 us
    all_to_all x1, waiting for transfers between devices, local(): lax.all_to_all(mid_part, ('shard', 'ctx'), split_axis=1, concat_axis=0, t...  247 us
    all_to_all x1, waiting for transfers between devices, local(): lax.all_to_all(expert_part, ('shard', 'ctx'), split_axis=1, concat_axis=0...  232 us
    psum x1, waiting for transfers between devices, local(): lax.psum((mixture_part, grad_part, score_part), 'tp')  141 us
    all_gather x1, blocking collectives, local(): lax.all_gather(router, ('shard', 'ctx'), axis=0, tiled=True)  135 us
    all_to_all x1, waiting for transfers between devices, local(): lax.all_to_all(send_grad, ('shard', 'ctx'), split_axis=0, concat_axis=1,...  128 us
    reduce_scatter x1, waiting for transfers between devices, local(): lax.psum_scatter(out_proj_grad, ('shard', 'ctx'), scatter_dimension=0, ti...  107 us
    unnamed x159, local copies, waits for them, and re-layouts  76.6 us
  transfers between devices with their start and end apart: 17, of which 14 were waited for; matrix products, arithmetic and copies ran while one was open for 12% of the time, Pallas kernels for 0%

commit v1 on v0

--- a/solution.py
+++ b/solution.py
@@ -7,6 +7,37 @@
 norm_eps = 1e-05
 rope_base = 10000.0
 masked_score = -1e30
+
+
+def obtain_windows(field, dimension_no, u):
+    latest, side_arr = (field.shape[:dimension_no], field.shape[dimension_no + 1 :])
+    tile_out = field.reshape(*latest, u, -1, *side_arr)
+    s_next = jnp.moveaxis(tile_out, dimension_no, 0)
+    return s_next
+
+
+def proceed_area_all(xs, dim_k):
+    odd = list(xs.shape[1:])
+    odd[dim_k] *= xs.shape[0]
+    step_out = jnp.moveaxis(xs, 0, dim_k).reshape(odd)
+    return step_out
+
+
+def _pair_quarters(inputs, mesh_name, w_in, own_rows=0):
+    arr_out = lax.axis_index(mesh_name)
+    x_new = lax.axis_size(mesh_name)
+    last, w1 = (x_new, arr_out)
+    frame_out = obtain_windows(inputs, w_in, last)
+    to_i = 1
+    ledger = [frame_out[w1]]
+    while to_i < last:
+        u_next = frame_out[w1 ^ to_i]
+        answer = lax.ppermute(u_next, mesh_name, [(dev_i, dev_i ^ to_i) for dev_i in range(last)])
+        ledger.append(answer)
+        to_i += 1
+    frame_out = jnp.stack(ledger, axis=0)[w1 ^ jnp.arange(last)]
+    z_new = proceed_area_all(frame_out, own_rows)
+    return z_new
 
 
 def places_info(order_row, length_row):
@@ -196,7 +227,7 @@
     out_grad_f = out_grad.astype(jnp.float32)
     back_rows, back_grads = (
         lax.all_to_all(expert_part, ("shard", "ctx"), split_axis=1, concat_axis=0, tiled=True),
-        lax.all_to_all(mid_part, ("shard", "ctx"), split_axis=1, concat_axis=0, tiled=True),
+        _pair_quarters(mid_part, ("shard", "ctx"), 1),
     )
     columns = back_rows.shape[-1]
     rows_y = back_rows.reshape(experts * capacity, columns)[slot_dest].reshape(

time: 2170 us -> 2180 us (level)
    ppermute x0 -> x15, waiting for transfers between devices: none -> 552 us  [_pair_quarters(): lax.ppermute(u_next, mesh_name, [(dev_i, dev_i ^ to_i) for dev_i in range...]
    all_to_all x1 -> x0, waiting for transfers between devices: 247 us -> none  [local(): lax.all_to_all(mid_part, ('shard', 'ctx'), split_axis=1, concat_axis=0, t...]
    all_to_all x1, waiting for transfers between devices: 232 us -> 0.01 us  [local(): lax.all_to_all(expert_part, ('shard', 'ctx'), split_axis=1, concat_axis=0...]
    ppermute x0 -> x15, starting transfers between devices: none -> 76.7 us  [_pair_quarters(): lax.ppermute(u_next, mesh_name, [(dev_i, dev_i ^ to_i) for dev_i in range...]
    psum x1, waiting for transfers between devices: 141 us -> 95 us  [local(): lax.psum((mixture_part, grad_part, score_part), 'tp')]
    all_to_all x1 -> x0, starting transfers between devices: 35.3 us -> none  [local(): lax.all_to_all(mid_part, ('shard', 'ctx'), split_axis=1, concat_axis=0, t...]
    all_to_all x1, starting transfers between devices: 66 us -> 35 us  [local(): lax.all_to_all(expert_part, ('shard', 'ctx'), split_axis=1, concat_axis=0...]
    all_to_all x1, waiting for transfers between devices: 128 us -> 97.9 us  [local(): lax.all_to_all(send_grad, ('shard', 'ctx'), split_axis=0, concat_axis=1,...]
  transfers between devices with their start and end apart: 17 -> 31, of which waited for: 14 -> 24; matrix products, arithmetic and copies ran while one was open for 12% -> 14% of each run, Pallas kernels for 0% -> 0%
where the time goes in v1:
time: 2180 us; the launch traced here: 2170 us
  waiting for transfers between devices  1390 us (64%)
  local copies, waits for them, and re-layouts  233 us (11%)
  blocking collectives  179 us (8%)
  starting transfers between devices  161 us (7%)
  matrix products  123 us (6%)
  other arithmetic  71.1 us (3%)
    ppermute x15, waiting for transfers between devices, _pair_quarters(): lax.ppermute(u_next, mesh_name, [(dev_i, dev_i ^ to_i) for dev_i in range...  552 us
    reduce_scatter x1, waiting for transfers between devices, local(): lax.psum_scatter(qkv_grad, ('shard', 'ctx'), scatter_dimension=0, tiled=T...  248 us
    all_gather x1, blocking collectives, local(): lax.all_gather(router, ('shard', 'ctx'), axis=0, tiled=True)  135 us
    reduce_scatter x1, waiting for transfers between devices, local(): lax.psum_scatter(out_proj_grad, ('shard', 'ctx'), scatter_dimension=0, ti...  107 us
    all_to_all x1, waiting for transfers between devices, local(): lax.all_to_all(send_grad, ('shard', 'ctx'), split_axis=0, concat_axis=1,...  97.9 us
    psum x1, waiting for transfers between devices, local(): lax.psum((mixture_part, grad_part, score_part), 'tp')  95 us
    unnamed x193, local copies, waits for them, and re-layouts  81.2 us
    ppermute x15, starting transfers between devices, _pair_quarters(): lax.ppermute(u_next, mesh_name, [(dev_i, dev_i ^ to_i) for dev_i in range...  76.7 us
  transfers between devices with their start and end apart: 31, of which 24 were waited for; matrix products, arithmetic and copies ran while one was open for 14% of the time, Pallas kernels for 0%

profile of v1, /device:TPU:0, one launch (start us, length us, event | category | flops | bytes accessed | tf_op | source)
XLA Modules:
  0.0 2168.5 jit_solution(3319242667779410353)
XLA Ops:
  10.3 23.8 %all_gather.18 = bf16[2048,4]{0,1:T(4,128)(2,1)S(1)} all-gather(bf16[128,4]{0,1:T(4,128)(2,1)} %param.14), channel_id=1, replica_groups=mesh['shard'=4,'ctx'=4,'tp'=2] {'shard','ctx'}, dimensions={0}, use_global_device_ids=true | all-gather | bytes 17408 | tf_op jit(solution)/shard_map/all_gather | solution.py:104
  37.0 76.5 %all-gather.6.cloned.1.call-done = bf16[6144,1024]{1,0:T(8,128)(2,1)} async-done(((bf16[384,1024]{1,0:T(8,128)(2,1)}), bf16[6144,1024]{1,0:T(8,128)(2,1)}) %all-gather.6.cloned.1.call-update) | async-done | bytes 12582928 | tf_op jit(solution)/shard_map/all_gather | solution.py:102
  113.5 6.3 fusion.78
  126.4 4.9 all-reduce.1
  143.1 18.8 all-gather.8.cloned.1.call-done
  168.6 45.6 %all-gather.10.cloned.1.call-done = bf16[2048,1024]{1,0:T(8,128)(2,1)} async-done(((bf16[128,1024]{1,0:T(8,128)(2,1)}), bf16[2048,1024]{1,0:T(8,128)(2,1)}) %all-gather.10.cloned.1.call-update) | async-done | bytes 4194320 | tf_op jit(solution)/shard_map/all_gather | solution.py:103
  214.3 4.9 fusion.83
  219.8 4.5 reduce-window.11
  225.1 6.4 scatter_custom_fusion
  231.6 37.8 %all-reduce.7.cloned.1.call-done = f32[192,2048]{1,0:T(8,128)} async-done(((f32[192,2048]{1,0:T(8,128)}), f32[192,2048]{1,0:T(8,128)}) %all-reduce.7.cloned.1.call-update) | async-done | bytes 1572880 | tf_op jit(solution)/shard_map/psum | solution.py:176
  272.4 8.6 gather_fusion
  281.1 7.1 broadcast_select_fusion
  288.2 5.8 all-to-all-start
  294.0 8.7 gather_fusion.2
  302.7 134.7 %all_gather.23 = bf16[2048,16]{0,1:T(8,128)(2,1)S(1)} all-gather(bf16[128,16]{0,1:T(8,128)(2,1)S(1)} %copy-done.81), channel_id=1, replica_groups=mesh['shard'=4,'ctx'=4,'tp'=2] {'shard','ctx'}, dimensions={0}, use_global_device_ids=true | all-gather | bytes 69632 | tf_op jit(solution)/shard_map/all_gather | solution.py:105
  441.8 6.2 scatter_custom_fusion.1
  448.1 7.7 fusion
  455.8 42.3 %all-to-all-start.2 = ((bf16[16,120,2048]{2,1,0:T(8,128)(2,1)}), bf16[16,120,2048]{2,1,0:T(8,128)(2,1)}, u32[]{:S(2)}, u32[]{:S(2)}) async-start(bf16[16,120,2048]{2,1,0:T(8,128)(2,1)} %fusion), calls=%async_computation.2 | async-start | bytes 15728640 | tf_op jit(solution)/shard_map/all_to_all | solution.py:205
  498.1 11.9 convolution_bitcast_fusion.4
  519.0 22.7 %copy.134 = f32[1,1920,2048]{2,0,1:T(1,128)} copy(f32[1,1920,2048]{2,1,0:T(8,128)S(1)} %convolution_bitcast_fusion) | data formatting | bytes 31457280 | tf_op jit(solution)/shard_map/erf,edf->erd/dot_general | solution.py:213
  541.7 97.9 %all-to-all-done.2 = bf16[16,120,2048]{2,1,0:T(8,128)(2,1)} async-done(((bf16[16,120,2048]{2,1,0:T(8,128)(2,1)}), bf16[16,120,2048]{2,1,0:T(8,128)(2,1)}, u32[]{:S(2)}, u32[]{:S(2)}) %all-to-all-start.2) | async-done | bytes 7864352 | tf_op jit(solution)/shard_map/all_to_all | solution.py:205
  639.6 35.0 %all-to-all-start.1 = ((f32[1,1920,2048]{2,0,1:T(1,128)}), f32[1,1920,2048]{2,0,1:T(1,128)}, u32[]{:S(2)}, u32[]{:S(2)}) async-start(f32[1,1920,2048]{2,0,1:T(1,128)} %copy.134), calls=%async_computation.1 | async-start | bytes 31457280 | tf_op jit(solution)/shard_map/all_to_all | solution.py:229
  675.2 10.2 fusion.31
  689.0 11.0 convolution_bitcast_fusion.2
  700.0 10.5 constant_dynamic-slice_fusion
  725.4 59.4 %collective-permute-done.1 = f32[1,120,2048]{2,1,0:T(8,128)} collective-permute-done((f32[1,120,2048]{2,1,0:T(8,128)}, f32[1,120,2048]{2,1,0:T(8,128)}, u32[]{:S(2)}, u32[]{:S(2)}) %collective-permute-start.1) | collective-permute-done | bytes 983072 | tf_op jit(solution)/shard_map/ppermute | solution.py:35
  787.1 39.5 %collective-permute-done.2 = f32[1,120,2048]{2,1,0:T(8,128)S(1)} collective-permute-done((f32[1,120,2048]{2,1,0:T(8,128)}, f32[1,120,2048]{2,1,0:T(8,128)S(1)}, u32[]{:S(2)}, u32[]{:S(2)}) %collective-permute-start.2) | collective-permute-done | bytes 983072 | tf_op jit(solution)/shard_map/ppermute | solution.py:35
  827.7 185.4 %collective-permute-done.3 = f32[1,120,2048]{2,1,0:T(8,128)S(1)} collective-permute-done((f32[1,120,2048]{2,1,0:T(8,128)S(1)}, f32[1,120,2048]{2,1,0:T(8,128)S(1)}, u32[]{:S(2)}, u32[]{:S(2)}) %collective-permute-start.3) | collective-permute-done | bytes 983072 | tf_op jit(solution)/shard_map/ppermute | solution.py:35
  1013.1 4.9 collective-permute-start.5
  1019.0 15.2 collective-permute-done.4
  1039.8 19.1 collective-permute-done.5
  1058.9 23.8 %collective-permute-start.7 = (f32[1,120,2048]{2,1,0:T(8,128)S(1)}, f32[1,120,2048]{2,1,0:T(8,128)S(1)}, u32[]{:S(2)}, u32[]{:S(2)}) collective-permute-start(f32[1,120,2048]{2,1,0:T(8,128)S(1)} %copy-done.40), channel_id=1, source_target_pairs={{0,16},{2,18},{4,20},{6,22},{8,24},{10,26},{12,28},{14,30},{16,0},... | collective-permute-start | bytes 2949128 | tf_op jit(solution)/shard_map/ppermute | solution.py:35
  1083.8 5.2 collective-permute-done.6
  1089.0 14.3 collective-permute-start.8
  1104.4 113.1 %collective-permute-done.7 = f32[1,120,2048]{2,1,0:T(8,128)S(1)} collective-permute-done((f32[1,120,2048]{2,1,0:T(8,128)S(1)}, f32[1,120,2048]{2,1,0:T(8,128)S(1)}, u32[]{:S(2)}, u32[]{:S(2)}) %collective-permute-start.7) | collective-permute-done | bytes 983072 | tf_op jit(solution)/shard_map/ppermute | solution.py:35
  1217.5 8.5 collective-permute-start.9
  1227.0 31.4 %collective-permute-done.8 = f32[1,120,2048]{2,1,0:T(8,128)S(1)} collective-permute-done((f32[1,120,2048]{2,1,0:T(8,128)S(1)}, f32[1,120,2048]{2,1,0:T(8,128)S(1)}, u32[]{:S(2)}, u32[]{:S(2)}) %collective-permute-start.8) | collective-permute-done | bytes 983072 | tf_op jit(solution)/shard_map/ppermute | solution.py:35
  1258.4 8.2 collective-permute-start.10
  1267.8 64.0 %collective-permute-done.9 = f32[1,120,2048]{2,1,0:T(8,128)S(1)} collective-permute-done((f32[1,120,2048]{2,1,0:T(8,128)S(1)}, f32[1,120,2048]{2,1,0:T(8,128)S(1)}, u32[]{:S(2)}, u32[]{:S(2)}) %collective-permute-start.9) | collective-permute-done | bytes 983072 | tf_op jit(solution)/shard_map/ppermute | solution.py:35
  1335.2 16.4 collective-permute-done.10
  1360.5 13.2 gather_fusion.3
  1373.7 18.2 gather_fusion.4
  1391.9 8.7 bitcast_reduce_fusion
  1400.6 18.8 copy.240
  1419.4 18.3 gather_fusion.1
  1437.8 8.6 fusion.2
  1446.6 5.1 psum.75
  1451.8 95.0 %all-reduce.11.cloned.1.call-done = (f32[192,2048]{1,0:T(8,128)}, f32[192,2048]{1,0:T(8,128)}) async-done(((f32[192,2048]{1,0:T(8,128)}, f32[192,2048]{1,0:T(8,128)}), (f32[192,2048]{1,0:T(8,128)}, f32[192,2048]{1,0:T(8,128)})) %all-reduce.11.cloned.1.call-update) | async-done | bytes 3145744 | tf_op jit(solution)/shard_map/psum | solution.py:243
  1565.5 5.0 fusion.21
  1582.4 21.1 reduce-scatter.9.cloned.1.call-done
  1607.6 4.9 all-reduce
  1616.1 28.4 %reduce-scatter.11.cloned.1.call-done = f32[192,1024]{1,0:T(8,128)} async-done(((f32[768,1024]{1,0:T(8,128)}), f32[192,1024]{1,0:T(8,128)}) %reduce-scatter.11.cloned.1.call-update) | async-done | bytes 786448 | tf_op jit(solution)/shard_map/reduce_scatter | solution.py:294
  1646.5 9.8 fusion.16
  1656.4 5.0 psum.79
  1661.4 29.4 %all-reduce.9.cloned.1.call-done = bf16[192,2048]{1,0:T(8,128)(2,1)} async-done(((bf16[192,2048]{1,0:T(8,128)(2,1)}), bf16[192,2048]{1,0:T(8,128)(2,1)}) %all-reduce.9.cloned.1.call-update) | async-done | bytes 786448 | tf_op jit(solution)/shard_map/psum | solution.py:319
  1695.9 6.0 fusion.81
  1703.0 10.4 convolution_bitcast_fusion.1
  1713.4 24.8 %copy.147 = f32[3,2048,1024]{2,1,0:T(8,128)} copy(f32[3,2048,1024]{1,2,0:T(8,128)} %convolution_bitcast_fusion.1) | data formatting | bytes 50331648 | tf_op jit(solution)/shard_map/td,tjh->jdh/transpose | solution.py:314
  1739.9 12.1 convolution_bitcast_fusion.3
  1752.0 16.5 copy.149
  1768.5 9.6 convolution_bitcast_fusion.5
  1781.2 25.6 %reduce-scatter.17.cloned.1.call-done = f32[128,16]{0,1:T(8,128)} async-done(((f32[2048,16]{0,1:T(8,128)}), f32[128,16]{0,1:T(8,128)}) %reduce-scatter.17.cloned.1.call-update) | async-done | bytes 8208 | tf_op jit(solution)/shard_map/reduce_scatter | solution.py:334
  1806.8 107.0 %reduce-scatter.15.cloned.1.call-done = f32[128,1024]{1,0:T(8,128)} async-done(((f32[2048,1024]{1,0:T(8,128)}), f32[128,1024]{1,0:T(8,128)}) %reduce-scatter.15.cloned.1.call-update) | async-done | bytes 524304 | tf_op jit(solution)/shard_map/reduce_scatter | solution.py:332
  1913.8 247.9 %reduce-scatter.13.cloned.1.call-done = f32[384,1024]{1,0:T(8,128)} async-done(((f32[6144,1024]{1,0:T(8,128)}), f32[384,1024]{1,0:T(8,128)}) %reduce-scatter.13.cloned.1.call-update) | async-done | bytes 1572880 | tf_op jit(solution)/shard_map/reduce_scatter | solution.py:331
  (338 shorter events, 145.0 us)
Async XLA Ops:
  7.2 507.5 %copy-start = (bf16[1,2048,512]{2,1,0:T(8,128)(2,1)S(1)}, bf16[1,2048,512]{2,1,0:T(8,128)(2,1)}, u32[]{:S(2)}) copy-start(bf16[1,2048,512]{2,1,0:T(8,128)(2,1)} %param.17) | copy-start | bytes 6291460
  7.2 106.3 %all-gather.6.cloned.1.call-start = ((), (), s32[]{:S(2)}) async-start(), calls=%async_computation.9 | async-start | bytes 13369344 | tf_op jit(solution)/shard_map/all_gather | solution.py:102
  7.9 132.1 %all-gather.12.cloned.1.call-start = ((), (), s32[]{:S(2)}) async-start(), calls=%async_computation.19 | async-start | bytes 1966080 | tf_op jit(solution)/shard_map/all_gather | solution.py:152
  35.5 98.0 %copy-start.46 = (f32[192,128]{1,0:T(8,128)}, f32[192,128]{1,0:T(8,128)S(1)}, u32[]{:S(2)}) copy-start(f32[192,128]{1,0:T(8,128)S(1)} %get-tuple-element.103) | copy-start | bytes 294916
  36.9 82.8 %copy-start.66 = (f32[192]{0:T(256)}, f32[192]{0:T(256)S(1)}, u32[]{:S(2)}) copy-start(f32[192]{0:T(256)S(1)} %add_rsqrt_fusion.3) | copy-start | bytes 2308
  37.0 82.8 %copy-start.50 = (f32[2048,1]{0,1:T(1,128)}, f32[2048,1]{0,1:T(1,128)S(1)}, u32[]{:S(2)}) copy-start(f32[2048,1]{0,1:T(1,128)S(1)} %get-tuple-element.109) | copy-start | bytes 24580
  37.0 400.5 %copy-start.54 = (f32[2048,1]{0,1:T(1,128)}, f32[2048,1]{0,1:T(1,128)S(1)}, u32[]{:S(2)}) copy-start(f32[2048,1]{0,1:T(1,128)S(1)} %get-tuple-element.106) | copy-start | bytes 24580
  122.0 39.8 %all-gather.8.cloned.1.call-start = ((), (), s32[]{:S(2)}) async-start(), calls=%async_computation.10 | async-start | bytes 1966080 | tf_op jit(solution)/shard_map/all_gather | solution.py:151
  134.1 30.4 %copy-start.20 = (bf16[192,8,128]{2,0,1:T(8,128)(2,1)}, bf16[192,8,128]{2,0,1:T(8,128)(2,1)S(1)}, u32[]{:S(2)}) copy-start(bf16[192,8,128]{2,0,1:T(8,128)(2,1)S(1)} %get-tuple-element.105) | copy-start | bytes 1179652
  137.3 77.0 %all-gather.10.cloned.1.call-start = ((), (), s32[]{:S(2)}) async-start(), calls=%async_computation.11 | async-start | bytes 4456448 | tf_op jit(solution)/shard_map/all_gather | solution.py:103
  137.9 131.5 %all-reduce.7.cloned.1.call-start = ((), (), s32[]{:S(2)}) async-start(), calls=%async_computation.12 | async-start | bytes 3145728 | tf_op jit(solution)/shard_map/psum | solution.py:176
  168.6 50.8 %copy-start.30 = (bf16[8,24,8,128]{3,2,1,0:T(8,128)(2,1)}, bf16[8,24,8,128]{3,2,1,0:T(8,128)(2,1)S(1)}, u32[]{:S(2)}) copy-start(bf16[8,24,8,128]{3,2,1,0:T(8,128)(2,1)S(1)} %fusion.57) | copy-start | bytes 1179652
  168.6 50.6 %copy-start.58 = (s32[192,8]{0,1:T(8,128)S(1)}, s32[192,8]{0,1:T(8,128)}, u32[]{:S(2)}) copy-start(s32[192,8]{0,1:T(8,128)} %param.18) | copy-start | bytes 18436
  168.6 100.8 %copy-start.7 = (bf16[192,2048]{1,0:T(8,128)(2,1)S(1)}, bf16[192,2048]{1,0:T(8,128)(2,1)}, u32[]{:S(2)}) copy-start(bf16[192,2048]{1,0:T(8,128)(2,1)} %param.11) | copy-start | bytes 2359300
  271.1 166.3 %copy-start.68 = (f32[192]{0:T(256)}, f32[192]{0:T(256)S(1)}, u32[]{:S(2)}) copy-start(f32[192]{0:T(256)S(1)} %add_rsqrt_fusion) | copy-start | bytes 2308
  288.2 167.6 %all-to-all-start = ((bf16[16,120,2048]{2,1,0:T(8,128)(2,1)}), bf16[16,120,2048]{2,1,0:T(8,128)(2,1)}, u32[]{:S(2)}, u32[]{:S(2)}) async-start(bf16[16,120,2048]{2,1,0:T(8,128)(2,1)} %broadcast_select_fusion), calls=%async_computation | async-start | bytes 15728640 | tf_op jit(solution)/shard_map/all_to_all | solution.py:204
  455.8 183.8 %all-to-all-start.2 = ((bf16[16,120,2048]{2,1,0:T(8,128)(2,1)}), bf16[16,120,2048]{2,1,0:T(8,128)(2,1)}, u32[]{:S(2)}, u32[]{:S(2)}) async-start(bf16[16,120,2048]{2,1,0:T(8,128)(2,1)} %fusion), calls=%async_computation.2 | async-start | bytes 15728640 | tf_op jit(solution)/shard_map/all_to_all | solution.py:205
  639.6 761.0 %all-to-all-start.1 = ((f32[1,1920,2048]{2,0,1:T(1,128)}), f32[1,1920,2048]{2,0,1:T(1,128)}, u32[]{:S(2)}, u32[]{:S(2)}) async-start(f32[1,1920,2048]{2,0,1:T(1,128)} %copy.134), calls=%async_computation.1 | async-start | bytes 31457280 | tf_op jit(solution)/shard_map/all_to_all | solution.py:229
  674.6 872.1 %all-reduce.11.cloned.1.call-start = ((), (), s32[]{:S(2)}) async-start(), calls=%async_computation.21 | async-start | bytes 6291456 | tf_op jit(solution)/shard_map/psum | solution.py:243
  710.6 12.0 collective-permute-start
  711.0 73.8 %collective-permute-start.1 = (f32[1,120,2048]{2,1,0:T(8,128)}, f32[1,120,2048]{2,1,0:T(8,128)}, u32[]{:S(2)}, u32[]{:S(2)}) collective-permute-start(f32[1,120,2048]{2,1,0:T(8,128)} %get-tuple-element.83), channel_id=1, source_target_pairs={{0,4},{2,6},{4,0},{6,2},{8,12},{10,14},{12,8},{14,10},{16,20},{18,... | collective-permute-start | bytes 2949128 | tf_op jit(solution)/shard_map/ppermute | solution.py:35
  712.8 72.0 %copy-start.43 = (f32[1,120,2048]{2,1,0:T(8,128)S(1)}, f32[1,120,2048]{2,1,0:T(8,128)}, u32[]{:S(2)}) copy-start(f32[1,120,2048]{2,1,0:T(8,128)} %get-tuple-element.81) | copy-start | bytes 2949124
  712.9 646.6 %collective-permute-start.14 = (f32[1,120,2048]{2,1,0:T(8,128)}, f32[1,120,2048]{2,1,0:T(8,128)S(1)}, u32[]{:S(2)}, u32[]{:S(2)}) collective-permute-start(f32[1,120,2048]{2,1,0:T(8,128)} %get-tuple-element.70), channel_id=1, source_target_pairs={{0,30},{2,28},{4,26},{6,24},{8,22},{10,20},{12,18},{14,16},{16,14}... | collective-permute-start | bytes 2949128 | tf_op jit(solution)/shard_map/ppermute | solution.py:35
  715.9 642.5 %collective-permute-start.13 = (f32[1,120,2048]{2,1,0:T(8,128)}, f32[1,120,2048]{2,1,0:T(8,128)S(1)}, u32[]{:S(2)}, u32[]{:S(2)}) collective-permute-start(f32[1,120,2048]{2,1,0:T(8,128)} %get-tuple-element.71), channel_id=1, source_target_pairs={{0,28},{2,30},{4,24},{6,26},{8,20},{10,22},{12,16},{14,18},{16,12}... | collective-permute-start | bytes 2949128 | tf_op jit(solution)/shard_map/ppermute | solution.py:35
  717.4 295.7 %copy-start.42 = (f32[1,120,2048]{2,1,0:T(8,128)S(1)}, f32[1,120,2048]{2,1,0:T(8,128)}, u32[]{:S(2)}) copy-start(f32[1,120,2048]{2,1,0:T(8,128)} %get-tuple-element.79) | copy-start | bytes 2949124
  717.4 640.0 %collective-permute-start.12 = (f32[1,120,2048]{2,1,0:T(8,128)}, f32[1,120,2048]{2,1,0:T(8,128)S(1)}, u32[]{:S(2)}, u32[]{:S(2)}) collective-permute-start(f32[1,120,2048]{2,1,0:T(8,128)} %get-tuple-element.72), channel_id=1, source_target_pairs={{0,26},{2,24},{4,30},{6,28},{8,18},{10,16},{12,22},{14,20},{16,10}... | collective-permute-start | bytes 2949128 | tf_op jit(solution)/shard_map/ppermute | solution.py:35
  722.6 311.7 %copy-start.41 = (f32[1,120,2048]{2,1,0:T(8,128)S(1)}, f32[1,120,2048]{2,1,0:T(8,128)}, u32[]{:S(2)}) copy-start(f32[1,120,2048]{2,1,0:T(8,128)} %get-tuple-element.78) | copy-start | bytes 2949124
  722.6 104.0 %collective-permute-start.2 = (f32[1,120,2048]{2,1,0:T(8,128)}, f32[1,120,2048]{2,1,0:T(8,128)S(1)}, u32[]{:S(2)}, u32[]{:S(2)}) collective-permute-start(f32[1,120,2048]{2,1,0:T(8,128)} %get-tuple-element.82), channel_id=1, source_target_pairs={{0,6},{2,4},{4,2},{6,0},{8,14},{10,12},{12,10},{14,8},{16,22},{18,... | collective-permute-start | bytes 2949128 | tf_op jit(solution)/shard_map/ppermute | solution.py:35
  784.8 274.1 %copy-start.40 = (f32[1,120,2048]{2,1,0:T(8,128)S(1)}, f32[1,120,2048]{2,1,0:T(8,128)}, u32[]{:S(2)}) copy-start(f32[1,120,2048]{2,1,0:T(8,128)} %get-tuple-element.77) | copy-start | bytes 2949124
  784.8 228.3 %collective-permute-start.3 = (f32[1,120,2048]{2,1,0:T(8,128)S(1)}, f32[1,120,2048]{2,1,0:T(8,128)S(1)}, u32[]{:S(2)}, u32[]{:S(2)}) collective-permute-start(f32[1,120,2048]{2,1,0:T(8,128)S(1)} %copy-done.43), channel_id=1, source_target_pairs={{0,8},{2,10},{4,12},{6,14},{8,0},{10,2},{12,4},{14,6},{16,24},{18,... | collective-permute-start | bytes 2949128 | tf_op jit(solution)/shard_map/ppermute | solution.py:35
  826.6 262.4 %copy-start.39 = (f32[1,120,2048]{2,1,0:T(8,128)S(1)}, f32[1,120,2048]{2,1,0:T(8,128)}, u32[]{:S(2)}) copy-start(f32[1,120,2048]{2,1,0:T(8,128)} %get-tuple-element.76) | copy-start | bytes 2949124
  826.6 207.7 %collective-permute-start.4 = (f32[1,120,2048]{2,1,0:T(8,128)}, f32[1,120,2048]{2,1,0:T(8,128)S(1)}, u32[]{:S(2)}, u32[]{:S(2)}) collective-permute-start(f32[1,120,2048]{2,1,0:T(8,128)} %get-tuple-element.80), channel_id=1, source_target_pairs={{0,10},{2,8},{4,14},{6,12},{8,2},{10,0},{12,6},{14,4},{16,26},{18,... | collective-permute-start | bytes 2949128 | tf_op jit(solution)/shard_map/ppermute | solution.py:35
  1013.1 204.4 %copy-start.38 = (f32[1,120,2048]{2,1,0:T(8,128)S(1)}, f32[1,120,2048]{2,1,0:T(8,128)}, u32[]{:S(2)}) copy-start(f32[1,120,2048]{2,1,0:T(8,128)} %get-tuple-element.75) | copy-start | bytes 2949124
  1013.1 45.8 %collective-permute-start.5 = (f32[1,120,2048]{2,1,0:T(8,128)S(1)}, f32[1,120,2048]{2,1,0:T(8,128)S(1)}, u32[]{:S(2)}, u32[]{:S(2)}) collective-permute-start(f32[1,120,2048]{2,1,0:T(8,128)S(1)} %copy-done.42), channel_id=1, source_target_pairs={{0,12},{2,14},{4,8},{6,10},{8,4},{10,6},{12,0},{14,2},{16,28},{18,... | collective-permute-start | bytes 2949128 | tf_op jit(solution)/shard_map/ppermute | solution.py:35
  1034.3 224.2 %copy-start.37 = (f32[1,120,2048]{2,1,0:T(8,128)S(1)}, f32[1,120,2048]{2,1,0:T(8,128)}, u32[]{:S(2)}) copy-start(f32[1,120,2048]{2,1,0:T(8,128)} %get-tuple-element.74) | copy-start | bytes 2949124
  1034.3 54.8 %collective-permute-start.6 = (f32[1,120,2048]{2,1,0:T(8,128)S(1)}, f32[1,120,2048]{2,1,0:T(8,128)S(1)}, u32[]{:S(2)}, u32[]{:S(2)}) collective-permute-start(f32[1,120,2048]{2,1,0:T(8,128)S(1)} %copy-done.41), channel_id=1, source_target_pairs={{0,14},{2,12},{4,10},{6,8},{8,6},{10,4},{12,2},{14,0},{16,30},{18,... | collective-permute-start | bytes 2949128 | tf_op jit(solution)/shard_map/ppermute | solution.py:35
  1058.9 272.9 %copy-start.36 = (f32[1,120,2048]{2,1,0:T(8,128)S(1)}, f32[1,120,2048]{2,1,0:T(8,128)}, u32[]{:S(2)}) copy-start(f32[1,120,2048]{2,1,0:T(8,128)} %get-tuple-element.73) | copy-start | bytes 2949124
  1058.9 158.6 %collective-permute-start.7 = (f32[1,120,2048]{2,1,0:T(8,128)S(1)}, f32[1,120,2048]{2,1,0:T(8,128)S(1)}, u32[]{:S(2)}, u32[]{:S(2)}) collective-permute-start(f32[1,120,2048]{2,1,0:T(8,128)S(1)} %copy-done.40), channel_id=1, source_target_pairs={{0,16},{2,18},{4,20},{6,22},{8,24},{10,26},{12,28},{14,30},{16,0},... | collective-permute-start | bytes 2949128 | tf_op jit(solution)/shard_map/ppermute | solution.py:35
  1089.0 169.4 %collective-permute-start.8 = (f32[1,120,2048]{2,1,0:T(8,128)S(1)}, f32[1,120,2048]{2,1,0:T(8,128)S(1)}, u32[]{:S(2)}, u32[]{:S(2)}) collective-permute-start(f32[1,120,2048]{2,1,0:T(8,128)S(1)} %copy-done.39), channel_id=1, source_target_pairs={{0,18},{2,16},{4,22},{6,20},{8,26},{10,24},{12,30},{14,28},{16,2},... | collective-permute-start | bytes 2949128 | tf_op jit(solution)/shard_map/ppermute | solution.py:35
  1217.5 114.3 %collective-permute-start.9 = (f32[1,120,2048]{2,1,0:T(8,128)S(1)}, f32[1,120,2048]{2,1,0:T(8,128)S(1)}, u32[]{:S(2)}, u32[]{:S(2)}) collective-permute-start(f32[1,120,2048]{2,1,0:T(8,128)S(1)} %copy-done.38), channel_id=1, source_target_pairs={{0,20},{2,22},{4,16},{6,18},{8,28},{10,30},{12,24},{14,26},{16,4},... | collective-permute-start | bytes 2949128 | tf_op jit(solution)/shard_map/ppermute | solution.py:35
  1258.4 93.2 %collective-permute-start.10 = (f32[1,120,2048]{2,1,0:T(8,128)S(1)}, f32[1,120,2048]{2,1,0:T(8,128)S(1)}, u32[]{:S(2)}, u32[]{:S(2)}) collective-permute-start(f32[1,120,2048]{2,1,0:T(8,128)S(1)} %copy-done.37), channel_id=1, source_target_pairs={{0,22},{2,20},{4,18},{6,16},{8,30},{10,28},{12,26},{14,24},{16,6},... | collective-permute-start | bytes 2949128 | tf_op jit(solution)/shard_map/ppermute | solution.py:35
  1331.8 24.5 %collective-permute-start.11 = (f32[1,120,2048]{2,1,0:T(8,128)S(1)}, f32[1,120,2048]{2,1,0:T(8,128)S(1)}, u32[]{:S(2)}, u32[]{:S(2)}) collective-permute-start(f32[1,120,2048]{2,1,0:T(8,128)S(1)} %copy-done.36), channel_id=1, source_target_pairs={{0,24},{2,26},{4,28},{6,30},{8,16},{10,18},{12,20},{14,22},{16,8},... | collective-permute-start | bytes 2949128 | tf_op jit(solution)/shard_map/ppermute | solution.py:35
  1419.4 18.3 copy-start.45
  1437.7 109.0 %copy-start.49 = (bf16[2048,16]{0,1:T(8,128)(2,1)S(1)}, bf16[2048,16]{0,1:T(8,128)(2,1)}, u32[]{:S(2)}) copy-start(bf16[2048,16]{0,1:T(8,128)(2,1)} %copy-done.48) | copy-start | bytes 196612
  1437.8 109.0 %copy-start.55 = (f32[2048,1]{0,1:T(1,128)S(1)}, f32[2048,1]{0,1:T(1,128)}, u32[]{:S(2)}) copy-start(f32[2048,1]{0,1:T(1,128)} %copy-done.54) | copy-start | bytes 24580
  1437.8 109.0 %copy-start.69 = (f32[192]{0:T(256)S(1)}, f32[192]{0:T(256)}, u32[]{:S(2)}) copy-start(f32[192]{0:T(256)} %copy-done.68) | copy-start | bytes 2308
  1446.4 100.4 %copy-start.6 = (f32[192,2048]{1,0:T(8,128)S(1)}, f32[192,2048]{1,0:T(8,128)}, u32[]{:S(2)}) copy-start(f32[192,2048]{1,0:T(8,128)} %copy-done.5) | copy-start | bytes 4718596
  1446.4 157.1 %reduce-scatter.9.cloned.1.call-start = ((), (), s32[]{:S(2)}) async-start(), calls=%async_computation.13 | async-start | bytes 3932160 | tf_op jit(solution)/shard_map/reduce_scatter | solution.py:291
  1565.4 79.1 %reduce-scatter.11.cloned.1.call-start = ((), (), s32[]{:S(2)}) async-start(), calls=%async_computation.14 | async-start | bytes 3932160 | tf_op jit(solution)/shard_map/reduce_scatter | solution.py:294
  1574.2 116.5 %all-reduce.9.cloned.1.call-start = ((), (), s32[]{:S(2)}) async-start(), calls=%async_computation.15 | async-start | bytes 1572864 | tf_op jit(solution)/shard_map/psum | solution.py:319
  1578.2 25.3 %copy-start.47 = (f32[192,128]{1,0:T(8,128)S(1)}, f32[192,128]{1,0:T(8,128)}, u32[]{:S(2)}) copy-start(f32[192,128]{1,0:T(8,128)} %copy-done.46) | copy-start | bytes 294916
  1578.9 26.1 %copy-start.17 = (f32[192,8,128]{2,1,0:T(8,128)S(1)}, f32[192,8,128]{2,1,0:T(8,128)}, u32[]{:S(2)}) copy-start(f32[192,8,128]{2,1,0:T(8,128)} %copy-done.16) | copy-start | bytes 2359300
  1578.9 26.2 %copy-start.63 = (f32[1024,1]{0,1:T(1,128)S(1)}, f32[1024,1]{0,1:T(1,128)}, u32[]{:S(2)}) copy-start(f32[1024,1]{0,1:T(1,128)} %copy-done.62) | copy-start | bytes 12292
  1578.9 26.2 %copy-start.73 = (f32[192]{0:T(256)S(1)}, f32[192]{0:T(256)}, u32[]{:S(2)}) copy-start(f32[192]{0:T(256)} %copy-done.72) | copy-start | bytes 2308
  1616.1 29.6 %copy-start.32 = (bf16[192,1,1024]{2,0,1:T(8,128)(2,1)}, bf16[192,1,1024]{2,0,1:T(8,128)(2,1)S(1)}, u32[]{:S(2)}) copy-start(bf16[192,1,1024]{2,0,1:T(8,128)(2,1)S(1)} %multiply_convert_fusion.4) | copy-start | bytes 1179652
  1646.4 44.4 %copy-start.8 = (bf16[192,2048]{1,0:T(8,128)(2,1)S(1)}, bf16[192,2048]{1,0:T(8,128)(2,1)}, u32[]{:S(2)}) copy-start(bf16[192,2048]{1,0:T(8,128)(2,1)} %param.11) | copy-start | bytes 2359300
  1646.4 44.4 %copy-start.51 = (f32[2048,1]{0,1:T(1,128)S(1)}, f32[2048,1]{0,1:T(1,128)}, u32[]{:S(2)}) copy-start(f32[2048,1]{0,1:T(1,128)} %copy-done.50) | copy-start | bytes 24580
  1646.4 44.4 %copy-start.67 = (f32[192]{0:T(256)S(1)}, f32[192]{0:T(256)}, u32[]{:S(2)}) copy-start(f32[192]{0:T(256)} %copy-done.66) | copy-start | bytes 2308
  1656.3 39.7 %copy-start.31 = (bf16[8,24,8,128]{3,2,1,0:T(8,128)(2,1)S(1)}, bf16[8,24,8,128]{3,2,1,0:T(8,128)(2,1)}, u32[]{:S(2)}) copy-start(bf16[8,24,8,128]{3,2,1,0:T(8,128)(2,1)} %copy-done.30) | copy-start | bytes 1179652
  1656.3 123.4 %reduce-scatter.19.cloned.1.call-start = ((), (), s32[]{:S(2)}) async-start(), calls=%async_computation.20 | async-start | bytes 1114112
  1694.0 112.8 %reduce-scatter.17.cloned.1.call-start = ((), (), s32[]{:S(2)}) async-start(), calls=%async_computation.18 | async-start | bytes 139264 | tf_op jit(solution)/shard_map/reduce_scatter | solution.py:334
  1695.9 218.0 %reduce-scatter.15.cloned.1.call-start = ((), (), s32[]{:S(2)}) async-start(), calls=%async_computation.17 | async-start | bytes 8912896 | tf_op jit(solution)/shard_map/reduce_scatter | solution.py:332
  1701.9 459.8 %reduce-scatter.13.cloned.1.call-start = ((), (), s32[]{:S(2)}) async-start(), calls=%async_computation.16 | async-start | bytes 26738688 | tf_op jit(solution)/shard_map/reduce_scatter | solution.py:331
  1768.5 393.3 %copy-start.1 = (bf16[1,2048,512]{2,1,0:T(8,128)(2,1)S(1)}, bf16[1,2048,512]{2,1,0:T(8,128)(2,1)}, u32[]{:S(2)}) copy-start(bf16[1,2048,512]{2,1,0:T(8,128)(2,1)} %param.17) | copy-start | bytes 6291460
  (52 other events, 257.3 us)
Sparse Core Ops, SparseCore 0:
  10.3 103.1 all-gather.5
  122.1 17.8 all-gather.11
  142.2 19.6 all-gather.7
  163.9 50.3 all-gather.9
  219.3 50.0 all-reduce.6
  1446.5 100.1 all-reduce.10
  1565.5 37.8 reduce-scatter.8
  1606.6 37.8 reduce-scatter.10
  1656.4 34.3 all-reduce.8
  1694.3 57.5 reduce-scatter.18
  1755.8 50.9 reduce-scatter.16
  1811.3 102.4 reduce-scatter.14
  1918.5 243.1 reduce-scatter.12
